TPU v7x, 128 devices: a whole 4x4x4 slice. The times are simulated.
128 devices in a mesh: replica: 4 (over z), shard: 16 (over y, x_lo, core), tensor: 2 (over x_hi).
Axes of the slice: x: 4 (x_hi: 2, x_lo: 2; x = x_hi * 2 + x_lo), y: 4, z: 4, core: 2. Of those that a mesh axis runs over, the one named last changes fastest.
Arguments:
- trained_up: bfloat16 [4, 1024, 4096], P('replica', None, 'tensor'), may hold values from -6 to 6
- trained_down: bfloat16 [4, 4096, 1024], P('replica', 'tensor'), may hold values from -6 to 6
- trained_embed: bfloat16 [4, 32768, 1024], P('replica', ('shard', 'tensor')), may hold values from -6 to 6
- trained_norm: bfloat16 [4, 2, 1024], P('replica'), may hold values from 0.099609375 to 1.8984375
- master_up: float32 [1024, 4096], P(('replica', 'shard', 'tensor')), may hold values from -6 to 6
- moment_up: float32 [1024, 4096], P(('replica', 'shard', 'tensor')), may hold values from -4 to 4
- master_down: float32 [2, 2048, 1024], P('tensor', ('replica', 'shard')), may hold values from -6 to 6
- moment_down: float32 [2, 2048, 1024], P('tensor', ('replica', 'shard')), may hold values from -4 to 4
- master_embed: float32 [32, 1024, 1024], P(('shard', 'tensor'), 'replica'), may hold values from -6 to 6
- moment_embed: float32 [32, 1024, 64], P(('shard', 'tensor'), 'replica'), may hold values from -4 to 4
- master_norm: float32 [2, 1024], replicated, may hold values from 0.1 to 1.9
- moment_norm: float32 [2, 1024], replicated, may hold values from -2 to 2
- embed_basis: float32 [1024, 64], replicated, may hold values from -0.1875 to 0.1875
Outputs:
- recast_up: bfloat16 [1024, 4096], P(None, 'tensor')
- recast_down: bfloat16 [4096, 1024], P('tensor')
- recast_embed: bfloat16 [32768, 1024], P(('shard', 'tensor'))
- recast_norm: bfloat16 [2, 1024], replicated
- stored_up: float32 [1024, 4096], P(('replica', 'shard', 'tensor'))
- velocity_up: float32 [1024, 4096], P(('replica', 'shard', 'tensor'))
- stored_down: float32 [2, 2048, 1024], P('tensor', ('replica', 'shard'))
- velocity_down: float32 [2, 2048, 1024], P('tensor', ('replica', 'shard'))
- stored_embed: float32 [32, 1024, 1024], P(('shard', 'tensor'), 'replica')
- velocity_embed: float32 [32, 1024, 64], P(('shard', 'tensor'), 'replica')
- stored_norm: float32 [2, 1024], replicated
- velocity_norm: float32 [2, 1024], replicated
All inputs are finite; a program needn't handle non-finite values.
Results may differ from a plain program's by a relative error of at most 0.012.
Values may be sent and summed in bfloat16 or wider, within the bound.
A program may use at most 128 MiB of HBM per device.

v0:
```python
import jax
import jax.numpy as jnp
from jax import lax
from jax.sharding import PartitionSpec as P


def outer_step(master, moment, summed, groups):
    difference = master - summed / groups
    velocity = 0.5 * moment + difference
    return (master - 0.7 * (difference + 0.5 * velocity), velocity)


def body(
    trained_up,
    trained_down,
    trained_embed,
    trained_norm,
    master_up,
    moment_up,
    master_down,
    moment_down,
    master_embed,
    moment_embed,
    master_norm,
    moment_norm,
    embed_basis,
):
    replicas = lax.axis_size("replica")
    shards = lax.axis_size("shard")
    tensors = lax.axis_size("tensor")
    shard_pos = lax.axis_index("shard")
    width = embed_basis.shape[0]
    rows_up = master_up.shape[0]
    half_cols = trained_up.shape[2]
    rows_down = master_down.shape[1]
    up_blocks = trained_up[0].reshape(replicas, shards, tensors, rows_up, half_cols)
    up_own = lax.dynamic_index_in_dim(up_blocks, shard_pos, 1, keepdims=False)
    down_blocks = trained_down[0].reshape(replicas, shards, rows_down, width)
    down_own = lax.dynamic_index_in_dim(down_blocks, shard_pos, 1, keepdims=False)
    up_summed, down_summed = (
        lax.psum_scatter(
            up_own.astype(jnp.float32).astype(jnp.bfloat16),
            "replica",
            scatter_dimension=0,
            tiled=True,
        ).astype(jnp.float32),
        lax.psum_scatter(
            down_own.astype(jnp.float32).astype(jnp.bfloat16),
            "replica",
            scatter_dimension=0,
            tiled=True,
        ).astype(jnp.float32),
    )
    up_summed = lax.all_to_all(up_summed, "tensor", split_axis=1, concat_axis=3, tiled=True)
    stored_up, velocity_up = outer_step(
        master_up, moment_up, up_summed.reshape(rows_up, half_cols * tensors), replicas
    )
    stored_down, velocity_down = outer_step(master_down, moment_down, down_summed, replicas)
    norm_summed = lax.psum(trained_norm[0].astype(jnp.float32), "replica")
    stored_norm, velocity_norm = outer_step(master_norm, moment_norm, norm_summed, replicas)
    embed_own = master_embed[0]
    rows_embed = embed_own.shape[0]
    embed_terms = trained_embed[0].reshape(replicas, rows_embed, width).astype(jnp.float32)
    embed_summed = lax.psum_scatter(
        embed_terms.astype(jnp.bfloat16), "replica", scatter_dimension=0, tiled=True
    ).astype(jnp.float32)[0]
    coefficient = jnp.dot(
        embed_own - embed_summed / replicas, embed_basis, precision=lax.Precision.HIGHEST
    )
    velocity_rows = 0.5 * moment_embed[0] + coefficient
    stored_rows = embed_own - 0.7 * jnp.dot(
        coefficient + 0.5 * velocity_rows, embed_basis.T, precision=lax.Precision.HIGHEST
    )
    up_piece = lax.all_to_all(
        stored_up.astype(jnp.bfloat16), "tensor", split_axis=1, concat_axis=0, tiled=True
    )
    down_piece = stored_down[0].astype(jnp.bfloat16)
    recast_up, recast_down = (
        lax.all_gather(up_piece, ("replica", "shard"), axis=0, tiled=True),
        lax.all_gather(down_piece, ("replica", "shard"), axis=0, tiled=True),
    )
    recast_embed = lax.all_gather(stored_rows.astype(jnp.bfloat16), "replica", axis=0, tiled=True)
    return (
        recast_up,
        recast_down,
        recast_embed,
        stored_norm.astype(jnp.bfloat16),
        stored_up,
        velocity_up,
        stored_down,
        velocity_down,
        stored_rows[None],
        velocity_rows[None],
        stored_norm,
        velocity_norm,
    )


def solution(mesh):
    in_specs = (
        P("replica", None, "tensor"),
        P("replica", "tensor", None),
        P("replica", ("shard", "tensor"), None),
        P("replica", None, None),
        P(("replica", "shard", "tensor"), None),
        P(("replica", "shard", "tensor"), None),
        P("tensor", ("replica", "shard"), None),
        P("tensor", ("replica", "shard"), None),
        P(("shard", "tensor"), "replica", None),
        P(("shard", "tensor"), "replica", None),
        P(),
        P(),
        P(),
    )
    out_specs = (
        P(None, "tensor"),
        P("tensor", None),
        P(("shard", "tensor"), None),
        P(),
        P(("replica", "shard", "tensor"), None),
        P(("replica", "shard", "tensor"), None),
        P("tensor", ("replica", "shard"), None),
        P("tensor", ("replica", "shard"), None),
        P(("shard", "tensor"), "replica", None),
        P(("shard", "tensor"), "replica", None),
        P(),
        P(),
    )
    return jax.shard_map(body, mesh=mesh, in_specs=in_specs, out_specs=out_specs, check_vma=False)
```

profile of v0, /device:TPU:1, one launch (start us, length us, event | category | flops | bytes accessed | tf_op | source)
XLA Modules:
  0.0 376.6 jit_solution(8853071086595991756)
XLA Ops:
  7.2 0.0 copy-start
  7.2 0.0 copy-start.1
  7.2 0.0 copy-start.4
  7.2 0.0 reduce-scatter.6.cloned.1.call-start
  7.3 0.0 copy-start.12
  7.3 0.7 reduce-scatter.6.cloned.1.call-update
  7.9 0.0 copy-start.7
  8.0 0.0 copy-start.8
  8.0 0.0 all-reduce.3.cloned.1.call-start
  8.0 1.7 copy_bitcast_fusion
  9.7 0.0 all-reduce.3.cloned.1.call-update
  9.7 0.0 reduce-scatter.4.cloned.1.call-start
  9.8 0.0 copy-start.11
  9.8 1.7 dynamic-slice_bitcast_fusion
  11.5 0.0 reduce-scatter.4.cloned.1.call-update
  11.5 0.0 all-gather.7.cloned.1.call-start
  11.6 32.1 %reduce-scatter.6.cloned.1.call-done = bf16[1,256,1024]{2,1,0:T(8,128)(2,1)} async-done(((bf16[4,256,1024]{2,1,0:T(8,128)(2,1)}), bf16[1,256,1024]{2,1,0:T(8,128)(2,1)}) %reduce-scatter.6.cloned.1.call-update) | async-done | bytes 524304 | tf_op jit(solution)/shard_map/reduce_scatter | solution.py:64
  43.6 0.0 copy-done
  43.6 0.0 copy-done.1
  43.6 2.2 fusion.1
  45.8 0.0 copy-done.4
  45.8 2.2 fusion.16
  48.0 0.0 all-gather.7.cloned.1.call-update
  48.1 0.0 all-gather.5.cloned.1.call-start
  48.1 0.0 copy-done.12
  48.1 0.6 dynamic-slice
  48.7 37.3 %all-reduce.3.cloned.1.call-done = bf16[4,2,8,2048]{3,2,0,1:T(8,128)(2,1)} async-done(((bf16[4,2,8,2048]{3,2,0,1:T(8,128)(2,1)}), bf16[4,2,8,2048]{3,2,0,1:T(8,128)(2,1)}) %all-reduce.3.cloned.1.call-update) | async-done | bytes 262160
  86.0 1.5 dynamic-slice_convert_fusion
  87.5 8.6 %all_to_all.28 = f32[1,2,8,2048]{3,2,0,1:T(8,128)S(1)} all-to-all(f32[1,2,8,2048]{3,2,0,1:T(8,128)S(1)} %dynamic-slice_convert_fusion), channel_id=1, replica_groups=mesh['replica'=4,'shard'=16,'tensor'=2] {'tensor'}, dimensions={1} | all-to-all | bytes 262144 | tf_op jit(solution)/shard_map/all_to_all | solution.py:54
  96.1 0.7 fusion.15
  96.9 7.5 %all_to_all.29 = bf16[8,2,2048]{2,0,1:T(8,128)(2,1)} all-to-all(bf16[8,2,2048]{2,0,1:T(8,128)(2,1)S(1)} %bitcast.53), channel_id=1, replica_groups=mesh['replica'=4,'shard'=16,'tensor'=2] {'tensor'}, dimensions={1} | all-to-all | bytes 131072 | tf_op jit(solution)/shard_map/all_to_all | solution.py:74
  104.4 0.0 all-gather.5.cloned.1.call-update
  104.4 0.0 all-gather.9.cloned.1.call-start
  104.4 5.8 %reduce-scatter.4.cloned.1.call-done = bf16[1,32,1024]{2,1,0:T(8,128)(2,1)} async-done(((bf16[4,32,1024]{2,1,0:T(8,128)(2,1)}), bf16[1,32,1024]{2,1,0:T(8,128)(2,1)}) %reduce-scatter.4.cloned.1.call-update) | async-done | bytes 65552 | tf_op jit(solution)/shard_map/reduce_scatter | solution.py:47
  110.3 0.0 copy-done.6
  110.3 1.6 fusion.14
  111.9 0.0 all-gather.9.cloned.1.call-update
  111.9 6.9 %psum.7 = f32[2,1024]{1,0:T(2,128)S(1)} all-reduce(f32[2,1024]{1,0:T(2,128)S(1)} %bitcast_convert_fusion), channel_id=1, replica_groups=mesh['replica'=4,'shard'=16,'tensor'=2] {'replica'}, use_global_device_ids=true, to_apply=%region_3.4 | all-reduce | flops 2048 | bytes 16384 | tf_op jit(solution)/shard_map/psum | solution.py:59
  118.9 0.6 fusion.13
  119.5 0.6 fusion.8
  120.2 25.0 %all-gather.7.cloned.1.call-done = bf16[1024,1024]{1,0:T(8,128)(2,1)} async-done(((bf16[256,1024]{1,0:T(8,128)(2,1)}), bf16[1024,1024]{1,0:T(8,128)(2,1)}) %all-gather.7.cloned.1.call-update) | async-done | bytes 2097168 | tf_op jit(solution)/shard_map/all_gather | solution.py:82
  145.2 108.0 %all-gather.5.cloned.1.call-done = bf16[1024,2048]{1,0:T(8,128)(2,1)} async-done(((bf16[16,2048]{1,0:T(8,128)(2,1)}), bf16[1024,2048]{1,0:T(8,128)(2,1)}) %all-gather.5.cloned.1.call-update) | async-done | bytes 4194320 | tf_op jit(solution)/shard_map/all_gather | solution.py:79
  253.2 107.3 %all-gather.9.cloned.1.call-done = bf16[1,2048,1024]{2,1,0:T(8,128)(2,1)} async-done(((bf16[1,32,1024]{2,1,0:T(8,128)(2,1)}), bf16[1,2048,1024]{2,1,0:T(8,128)(2,1)}) %all-gather.9.cloned.1.call-update) | async-done | bytes 4194320 | tf_op jit(solution)/shard_map/all_gather | solution.py:80
  360.4 4.9 %copy.39 = bf16[1024,2048]{1,0:T(8,128)(2,1)} copy(bf16[1024,2048]{1,0:T(8,128)(2,1)} %all-gather.5.cloned.1.call-done) | data formatting | bytes 8388608
  365.4 0.0 copy-done.2
  365.4 2.1 copy.40
  367.5 1.0 copy-done.3
  368.5 1.3 copy.41
  (14 shorter events, 0.0 us)
Async XLA Ops:
  7.2 36.5 %copy-start = (f32[1024,64]{0,1:T(8,128)S(1)}, f32[1024,64]{0,1:T(8,128)}, u32[]{:S(2)}) copy-start(f32[1024,64]{0,1:T(8,128)} %param.25) | copy-start | bytes 786436
  7.2 36.5 %copy-start.1 = (f32[1,256,1024]{2,1,0:T(8,128)S(1)}, f32[1,256,1024]{2,1,0:T(8,128)}, u32[]{:S(2)}) copy-start(f32[1,256,1024]{2,1,0:T(8,128)} %param.21) | copy-start | bytes 3145732
  7.2 38.6 %copy-start.4 = (f32[1,256,64]{1,2,0:T(8,128)S(1)}, f32[1,256,64]{1,2,0:T(8,128)}, u32[]{:S(2)}) copy-start(f32[1,256,64]{1,2,0:T(8,128)} %param.22) | copy-start | bytes 196612
  7.2 36.4 %reduce-scatter.6.cloned.1.call-start = ((), (), s32[]{:S(2)}) async-start(), calls=%async_computation.6 | async-start | bytes 2621440 | tf_op jit(solution)/shard_map/reduce_scatter | solution.py:64
  7.3 40.9 %copy-start.12 = (u32[128]{0:T(128)S(1)}, u32[128]{0:T(128)}, u32[]{:S(2)}) copy-start(u32[128]{0:T(128)} %constant.47) | copy-start | bytes 1540
  7.9 88.2 %copy-start.7 = (f32[8,4096]{1,0:T(8,128)S(1)}, f32[8,4096]{1,0:T(8,128)}, u32[]{:S(2)}) copy-start(f32[8,4096]{1,0:T(8,128)} %param.17) | copy-start | bytes 393220
  8.0 88.2 %copy-start.8 = (f32[8,4096]{1,0:T(8,128)S(1)}, f32[8,4096]{1,0:T(8,128)}, u32[]{:S(2)}) copy-start(f32[8,4096]{1,0:T(8,128)} %param.18) | copy-start | bytes 393220
  8.0 78.0 %all-reduce.3.cloned.1.call-start = ((), (), s32[]{:S(2)}) async-start(), calls=%async_computation.9 | async-start | bytes 524288
  9.7 100.6 %copy-start.5 = (f32[1,32,1024]{2,1,0:T(8,128)S(1)}, f32[1,32,1024]{2,1,0:T(8,128)}, u32[]{:S(2)}) copy-start(f32[1,32,1024]{2,1,0:T(8,128)} %param.19) | copy-start | bytes 393220
  9.7 100.6 %copy-start.6 = (f32[1,32,1024]{2,1,0:T(8,128)S(1)}, f32[1,32,1024]{2,1,0:T(8,128)}, u32[]{:S(2)}) copy-start(f32[1,32,1024]{2,1,0:T(8,128)} %param.20) | copy-start | bytes 393220
  9.7 100.6 %reduce-scatter.4.cloned.1.call-start = ((), (), s32[]{:S(2)}) async-start(), calls=%async_computation.5 | async-start | bytes 327680 | tf_op jit(solution)/shard_map/reduce_scatter | solution.py:47
  9.8 102.1 %copy-start.11 = (bf16[1,2,1024]{2,1,0:T(2,128)(2,1)S(1)}, bf16[1,2,1024]{2,1,0:T(2,128)(2,1)}, u32[]{:S(2)}) copy-start(bf16[1,2,1024]{2,1,0:T(2,128)(2,1)} %param.16) | copy-start | bytes 12292
  11.5 107.4 %copy-start.9 = (f32[2,1024]{1,0:T(2,128)S(1)}, f32[2,1024]{1,0:T(2,128)}, u32[]{:S(2)}) copy-start(f32[2,1024]{1,0:T(2,128)} %param.23) | copy-start | bytes 24580
  11.5 107.4 %copy-start.10 = (f32[2,1024]{1,0:T(2,128)S(1)}, f32[2,1024]{1,0:T(2,128)}, u32[]{:S(2)}) copy-start(f32[2,1024]{1,0:T(2,128)} %param.24) | copy-start | bytes 24580
  11.5 133.6 %all-gather.7.cloned.1.call-start = ((), (), s32[]{:S(2)}) async-start(), calls=%async_computation.7 | async-start | bytes 2621440 | tf_op jit(solution)/shard_map/all_gather | solution.py:82
  48.1 205.1 %all-gather.5.cloned.1.call-start = ((), (), s32[]{:S(2)}) async-start(), calls=%async_computation.4 | async-start | bytes 4259840 | tf_op jit(solution)/shard_map/all_gather | solution.py:79
  104.4 256.0 %all-gather.9.cloned.1.call-start = ((), (), s32[]{:S(2)}) async-start(), calls=%async_computation.8 | async-start | bytes 4259840 | tf_op jit(solution)/shard_map/all_gather | solution.py:80
  360.4 4.9 %copy-start.2 = (bf16[1,2048,1024]{2,1,0:T(8,128)(2,1)S(1)}, bf16[1,2048,1024]{2,1,0:T(8,128)(2,1)}, u32[]{:S(2)}) copy-start(bf16[1,2048,1024]{2,1,0:T(8,128)(2,1)} %all-gather.9.cloned.1.call-done) | copy-start | bytes 12582916
  365.4 3.1 copy-start.3
Sparse Core Ops, SparseCore 0:
  10.4 33.1 reduce-scatter.5
  46.7 39.3 all-reduce.2
  89.0 21.2 reduce-scatter.3
  112.5 32.6 all-gather.6
  146.9 106.2 all-gather.4
  255.4 104.9 all-gather.8
where the time goes:
time: 377 us
  waiting for transfers between devices  316 us (84%)
  blocking collectives  23 us (6%)
  between operations  14.3 us (4%)
  local copies, waits for them, and re-layouts  13.4 us (4%)
  other arithmetic  5.09 us (1%)
  matrix products  4.38 us (1%)
    all_gather x1, waiting for transfers between devices, body(): lax.all_gather(up_piece, ('replica', 'shard'), axis=0, tiled=True)  108 us
    all_gather x1, waiting for transfers between devices, body(): lax.all_gather(down_piece, ('replica', 'shard'), axis=0, tiled=True)  107 us
    unnamed x7, waiting for transfers between devices  38.1 us
    reduce_scatter x1, waiting for transfers between devices, body(): lax.psum_scatter(embed_terms.astype(jnp.bfloat16), 'replica', scatter_dim...  32.1 us
    all_gather x1, waiting for transfers between devices, body(): lax.all_gather(stored_rows.astype(jnp.bfloat16), 'replica', axis=0, tiled...  25 us
    unnamed x30, local copies, waits for them, and re-layouts  10 us
    all_to_all x1, blocking collectives, body(): lax.all_to_all(up_summed, 'tensor', split_axis=1, concat_axis=3, tiled=True)  8.59 us
  transfers between devices with their start and end apart: 6, of which 6 were waited for; matrix products, arithmetic and copies ran while one was open for 4% of the time, Pallas kernels for 0%

commit v1 on v0

--- a/solution.py
+++ b/solution.py
@@ -77,7 +77,15 @@
     down_piece = stored_down[0].astype(jnp.bfloat16)
     recast_up, recast_down = (
         lax.all_gather(up_piece, ("replica", "shard"), axis=0, tiled=True),
-        lax.all_gather(down_piece, ("replica", "shard"), axis=0, tiled=True),
+        jnp.concatenate(
+            lax.all_to_all(
+                jnp.stack([down_piece] * lax.axis_size(("replica", "shard"))),
+                ("replica", "shard"),
+                0,
+                0,
+            ),
+            axis=0,
+        ),
     )
     recast_embed = lax.all_gather(stored_rows.astype(jnp.bfloat16), "replica", axis=0, tiled=True)
     return (

time: 377 us -> 315 us (0.84)
  waiting for transfers between devices: 316 us -> 191 us
  blocking collectives: 23 us -> 72.7 us
  starting transfers between devices: 0.24 us -> 9.87 us
  local copies, waits for them, and re-layouts: 13.4 us -> 17.5 us
    all_gather x1 -> x0, waiting for transfers between devices: 107 us -> none  [body(): lax.all_gather(down_piece, ('replica', 'shard'), axis=0, tiled=True)]
    psum x1, blocking collectives: 6.93 us -> 56.6 us  [body(): norm_summed = lax.psum(trained_norm[0].astype(jnp.float32), 'replica')]
    all_gather x1, waiting for transfers between devices: 25 us -> 8.55 us  [body(): lax.all_gather(stored_rows.astype(jnp.bfloat16), 'replica', axis=0, tiled...]
    all_to_all x0 -> x1, starting transfers between devices: none -> 9.67 us  [body(): lax.all_to_all(jnp.stack([down_piece] * lax.axis_size(('replica', 'shard'...]
    unnamed x30 -> x28, local copies, waits for them, and re-layouts: 10 us -> 11.5 us
    unnamed x7 -> x6, waiting for transfers between devices: 38.1 us -> 38 us
  transfers between devices with their start and end apart: 6 -> 6, of which waited for: 6 -> 5; matrix products, arithmetic and copies ran while one was open for 4% -> 5% of each run, Pallas kernels for 0% -> 0%
where the time goes in v1:
time: 315 us
  waiting for transfers between devices  191 us (61%)
  blocking collectives  72.7 us (23%)
  local copies, waits for them, and re-layouts  17.5 us (6%)
  between operations  13.9 us (4%)
  starting transfers between devices  9.87 us (3%)
  other arithmetic  5.08 us (2%)
  matrix products  4.38 us (1%)
    all_gather x1, waiting for transfers between devices, body(): lax.all_gather(up_piece, ('replica', 'shard'), axis=0, tiled=True)  107 us
    psum x1, blocking collectives, body(): norm_summed = lax.psum(trained_norm[0].astype(jnp.float32), 'replica')  56.6 us
    unnamed x6, waiting for transfers between devices  38 us
    reduce_scatter x1, waiting for transfers between devices, body(): lax.psum_scatter(embed_terms.astype(jnp.bfloat16), 'replica', scatter_dim...  32.1 us
    unnamed x28, local copies, waits for them, and re-layouts  11.5 us
    all_to_all x1, starting transfers between devices, body(): lax.all_to_all(jnp.stack([down_piece] * lax.axis_size(('replica', 'shard'...  9.67 us
    all_to_all x1, blocking collectives, body(): lax.all_to_all(up_summed, 'tensor', split_axis=1, concat_axis=3, tiled=True)  8.59 us
    all_gather x1, waiting for transfers between devices, body(): lax.all_gather(stored_rows.astype(jnp.bfloat16), 'replica', axis=0, tiled...  8.55 us
  transfers between devices with their start and end apart: 6, of which 5 were waited for; matrix products, arithmetic and copies ran while one was open for 5% of the time, Pallas kernels for 0%

profile of v1, /device:TPU:1, one launch (start us, length us, event | category | flops | bytes accessed | tf_op | source)
XLA Modules:
  0.0 314.8 jit_solution(9496992198973500709)
XLA Ops:
  7.2 0.0 copy-start
  7.2 0.0 copy-start.1
  7.2 0.0 copy-start.3
  7.2 0.0 reduce-scatter.6.cloned.1.call-start
  7.3 0.0 copy-start.11
  7.3 0.7 reduce-scatter.6.cloned.1.call-update
  7.9 0.0 copy-start.6
  8.0 0.0 copy-start.7
  8.0 0.0 all-reduce.3.cloned.1.call-start
  8.0 1.7 copy_bitcast_fusion
  9.7 0.0 all-reduce.3.cloned.1.call-update
  9.7 0.0 reduce-scatter.4.cloned.1.call-start
  9.8 1.7 dynamic-slice_bitcast_fusion
  11.5 0.0 reduce-scatter.4.cloned.1.call-update
  11.5 0.0 all-gather.5.cloned.1.call-start
  11.6 32.1 %reduce-scatter.6.cloned.1.call-done = bf16[1,256,1024]{2,1,0:T(8,128)(2,1)} async-done(((bf16[4,256,1024]{2,1,0:T(8,128)(2,1)}), bf16[1,256,1024]{2,1,0:T(8,128)(2,1)}) %reduce-scatter.6.cloned.1.call-update) | async-done | bytes 524304 | tf_op jit(solution)/shard_map/reduce_scatter | solution.py:64
  43.6 0.0 copy-done
  43.6 0.0 copy-done.1
  43.6 2.2 fusion.1
  45.8 0.0 copy-done.3
  45.8 2.2 fusion.15
  48.0 0.0 all-gather.5.cloned.1.call-update
  48.1 0.0 all-gather.3.cloned.1.call-start
  48.1 0.0 copy-done.11
  48.1 0.6 dynamic-slice
  48.7 37.3 %all-reduce.3.cloned.1.call-done = bf16[4,2,8,2048]{3,2,0,1:T(8,128)(2,1)} async-done(((bf16[4,2,8,2048]{3,2,0,1:T(8,128)(2,1)}), bf16[4,2,8,2048]{3,2,0,1:T(8,128)(2,1)}) %all-reduce.3.cloned.1.call-update) | async-done | bytes 262160
  86.0 1.5 dynamic-slice_convert_fusion
  87.5 8.6 %all_to_all.33 = f32[1,2,8,2048]{3,2,0,1:T(8,128)S(1)} all-to-all(f32[1,2,8,2048]{3,2,0,1:T(8,128)S(1)} %dynamic-slice_convert_fusion), channel_id=1, replica_groups=mesh['replica'=4,'shard'=16,'tensor'=2] {'tensor'}, dimensions={1} | all-to-all | bytes 262144 | tf_op jit(solution)/shard_map/all_to_all | solution.py:54
  96.1 0.0 copy-done.6
  96.1 0.0 copy-done.7
  96.1 0.7 fusion.14
  96.9 7.5 %all_to_all.34 = bf16[8,2,2048]{2,0,1:T(8,128)(2,1)} all-to-all(bf16[8,2,2048]{2,0,1:T(8,128)(2,1)S(1)} %bitcast.54), channel_id=1, replica_groups=mesh['replica'=4,'shard'=16,'tensor'=2] {'tensor'}, dimensions={1} | all-to-all | bytes 131072 | tf_op jit(solution)/shard_map/all_to_all | solution.py:74
  104.4 0.0 all-gather.3.cloned.1.call-update
  104.4 5.9 %reduce-scatter.4.cloned.1.call-done = bf16[1,32,1024]{2,1,0:T(8,128)(2,1)} async-done(((bf16[4,32,1024]{2,1,0:T(8,128)(2,1)}), bf16[1,32,1024]{2,1,0:T(8,128)(2,1)}) %reduce-scatter.4.cloned.1.call-update) | async-done | bytes 65552 | tf_op jit(solution)/shard_map/reduce_scatter | solution.py:47
  110.3 0.0 copy-done.5
  110.3 1.6 convert_bitcast_fusion
  111.9 2.5 stack.5
  114.4 9.7 %all-to-all-start.2 = ((bf16[64,32,1024]{2,1,0:T(8,128)(2,1)}), bf16[64,32,1024]{2,1,0:T(8,128)(2,1)}, u32[]{:S(2)}, u32[]{:S(2)}) async-start(bf16[64,32,1024]{2,1,0:T(8,128)(2,1)} %stack.5), calls=%async_computation.3 | async-start | bytes 8388608 | tf_op jit(solution)/shard_map/all_to_all | solution.py:81
  124.1 0.0 copy-done.10
  124.1 56.6 %psum.7 = f32[2,1024]{1,0:T(2,128)S(1)} all-reduce(f32[2,1024]{1,0:T(2,128)S(1)} %bitcast_convert_fusion), channel_id=1, replica_groups=mesh['replica'=4,'shard'=16,'tensor'=2] {'replica'}, use_global_device_ids=true, to_apply=%region_3.4 | all-reduce | flops 2048 | bytes 16384 | tf_op jit(solution)/shard_map/psum | solution.py:59
  180.7 0.6 fusion.13
  181.4 0.6 fusion.8
  182.0 0.0 all-to-all-done.2
  182.0 8.6 %all-gather.5.cloned.1.call-done = bf16[1024,1024]{1,0:T(8,128)(2,1)} async-done(((bf16[256,1024]{1,0:T(8,128)(2,1)}), bf16[1024,1024]{1,0:T(8,128)(2,1)}) %all-gather.5.cloned.1.call-update) | async-done | bytes 2097168 | tf_op jit(solution)/shard_map/all_gather | solution.py:90
  190.6 106.8 %all-gather.3.cloned.1.call-done = bf16[1024,2048]{1,0:T(8,128)(2,1)} async-done(((bf16[16,2048]{1,0:T(8,128)(2,1)}), bf16[1024,2048]{1,0:T(8,128)(2,1)}) %all-gather.3.cloned.1.call-update) | async-done | bytes 4194320 | tf_op jit(solution)/shard_map/all_gather | solution.py:79
  297.4 4.8 %copy.39 = bf16[1024,2048]{1,0:T(8,128)(2,1)} copy(bf16[1024,2048]{1,0:T(8,128)(2,1)} %all-gather.3.cloned.1.call-done) | data formatting | bytes 8388608
  302.2 4.8 %copy.40 = bf16[2048,1024]{1,0:T(8,128)(2,1)} copy(bf16[2048,1024]{1,0:T(8,128)(2,1)} %bitcast.11) | data formatting | bytes 8388608
  307.0 1.3 copy.41
  (12 shorter events, 0.0 us)
Async XLA Ops:
  7.2 36.5 %copy-start = (f32[1024,64]{0,1:T(8,128)S(1)}, f32[1024,64]{0,1:T(8,128)}, u32[]{:S(2)}) copy-start(f32[1024,64]{0,1:T(8,128)} %param.25) | copy-start | bytes 786436
  7.2 36.5 %copy-start.1 = (f32[1,256,1024]{2,1,0:T(8,128)S(1)}, f32[1,256,1024]{2,1,0:T(8,128)}, u32[]{:S(2)}) copy-start(f32[1,256,1024]{2,1,0:T(8,128)} %param.21) | copy-start | bytes 3145732
  7.2 38.6 %copy-start.3 = (f32[1,256,64]{1,2,0:T(8,128)S(1)}, f32[1,256,64]{1,2,0:T(8,128)}, u32[]{:S(2)}) copy-start(f32[1,256,64]{1,2,0:T(8,128)} %param.22) | copy-start | bytes 196612
  7.2 36.4 %reduce-scatter.6.cloned.1.call-start = ((), (), s32[]{:S(2)}) async-start(), calls=%async_computation.7 | async-start | bytes 2621440 | tf_op jit(solution)/shard_map/reduce_scatter | solution.py:64
  7.3 40.9 %copy-start.11 = (u32[128]{0:T(128)S(1)}, u32[128]{0:T(128)}, u32[]{:S(2)}) copy-start(u32[128]{0:T(128)} %constant.47) | copy-start | bytes 1540
  7.9 88.2 %copy-start.6 = (f32[8,4096]{1,0:T(8,128)S(1)}, f32[8,4096]{1,0:T(8,128)}, u32[]{:S(2)}) copy-start(f32[8,4096]{1,0:T(8,128)} %param.17) | copy-start | bytes 393220
  8.0 88.2 %copy-start.7 = (f32[8,4096]{1,0:T(8,128)S(1)}, f32[8,4096]{1,0:T(8,128)}, u32[]{:S(2)}) copy-start(f32[8,4096]{1,0:T(8,128)} %param.18) | copy-start | bytes 393220
  8.0 78.0 %all-reduce.3.cloned.1.call-start = ((), (), s32[]{:S(2)}) async-start(), calls=%async_computation.9 | async-start | bytes 524288
  9.7 100.6 %copy-start.4 = (f32[1,32,1024]{2,1,0:T(8,128)S(1)}, f32[1,32,1024]{2,1,0:T(8,128)}, u32[]{:S(2)}) copy-start(f32[1,32,1024]{2,1,0:T(8,128)} %param.19) | copy-start | bytes 393220
  9.7 100.6 %copy-start.5 = (f32[1,32,1024]{2,1,0:T(8,128)S(1)}, f32[1,32,1024]{2,1,0:T(8,128)}, u32[]{:S(2)}) copy-start(f32[1,32,1024]{2,1,0:T(8,128)} %param.20) | copy-start | bytes 393220
  9.7 100.6 %reduce-scatter.4.cloned.1.call-start = ((), (), s32[]{:S(2)}) async-start(), calls=%async_computation.6 | async-start | bytes 327680 | tf_op jit(solution)/shard_map/reduce_scatter | solution.py:47
  11.5 179.0 %all-gather.5.cloned.1.call-start = ((), (), s32[]{:S(2)}) async-start(), calls=%async_computation.8 | async-start | bytes 2621440 | tf_op jit(solution)/shard_map/all_gather | solution.py:90
  48.1 249.3 %all-gather.3.cloned.1.call-start = ((), (), s32[]{:S(2)}) async-start(), calls=%async_computation.5 | async-start | bytes 4259840 | tf_op jit(solution)/shard_map/all_gather | solution.py:79
  114.4 9.7 %copy-start.10 = (bf16[1,2,1024]{2,1,0:T(2,128)(2,1)S(1)}, bf16[1,2,1024]{2,1,0:T(2,128)(2,1)}, u32[]{:S(2)}) copy-start(bf16[1,2,1024]{2,1,0:T(2,128)(2,1)} %param.16) | copy-start | bytes 12292
  114.4 66.3 %copy-start.8 = (f32[2,1024]{1,0:T(2,128)S(1)}, f32[2,1024]{1,0:T(2,128)}, u32[]{:S(2)}) copy-start(f32[2,1024]{1,0:T(2,128)} %param.23) | copy-start | bytes 24580
  114.4 66.3 %copy-start.9 = (f32[2,1024]{1,0:T(2,128)S(1)}, f32[2,1024]{1,0:T(2,128)}, u32[]{:S(2)}) copy-start(f32[2,1024]{1,0:T(2,128)} %param.24) | copy-start | bytes 24580
  114.4 67.6 %all-to-all-start.2 = ((bf16[64,32,1024]{2,1,0:T(8,128)(2,1)}), bf16[64,32,1024]{2,1,0:T(8,128)(2,1)}, u32[]{:S(2)}, u32[]{:S(2)}) async-start(bf16[64,32,1024]{2,1,0:T(8,128)(2,1)} %stack.5), calls=%async_computation.3 | async-start | bytes 8388608 | tf_op jit(solution)/shard_map/all_to_all | solution.py:81
  302.2 4.8 %copy-start.2 = (bf16[1024,1024]{1,0:T(8,128)(2,1)S(1)}, bf16[1024,1024]{1,0:T(8,128)(2,1)}, u32[]{:S(2)}) copy-start(bf16[1024,1024]{1,0:T(8,128)(2,1)} %all-gather.5.cloned.1.call-done) | copy-start | bytes 6291460
Sparse Core Ops, SparseCore 0:
  10.4 33.1 reduce-scatter.5
  46.7 39.3 all-reduce.2
  89.0 21.2 reduce-scatter.3
  112.5 78.0 all-gather.4
  192.2 105.1 all-gather.2
